TPU v7x, 512 devices: a whole 4x4x16 slice. The times are simulated.
512 devices in a mesh: tensor: 8 (over y, core), adapter: 16 (over z), dp: 4 (over x).
Axes of the slice: x: 4, y: 4, z: 16, core: 2. Of those that a mesh axis runs over, the one named last changes fastest.
Arguments:
- tokens: bfloat16 [16384, 8192], P(('adapter', 'dp'), 'tensor'), may hold values from -6 to 6
- base_projection_weight: bfloat16 [8192, 4096], P('tensor', 'dp'), may hold values from -0.0625 to 0.0625
- adapter_down_weight: bfloat16 [32, 8192, 64], P('adapter', 'tensor'), may hold values from -0.0625 to 0.0625
- adapter_up_weight: bfloat16 [32, 64, 4096], P('adapter', None, 'tensor'), may hold values from -0.75 to 0.75
- adapter_choice_index: int32 [512, 3], P(('adapter', 'dp')), may hold values from 0 to 31, as said below
Outputs:
- adapted: bfloat16 [16384, 4096], P(('adapter', 'dp'), 'tensor')
Inputs may be any that keep to these rules, and one draw needn't show every extreme that they name: `adapter_choice_index`: adapter a is held by index a // 2 of the adapter axis (its owner). Among the 24 entries of the sequences of one device, at most 3 name adapters of one owner, and in every draw one owner is named exactly 3 times by the entries of every device.
All inputs are finite; a program needn't handle non-finite values.
Results may differ from a plain program's by a relative error of at most 0.02.
Values may be sent and summed in bfloat16 or wider, within the bound.
No kernel may reach another device: no remote copies, remote signals or barrier semaphores. Data moves between devices by JAX's collectives and lax.ppermute only.
A program may use at most 64 MiB of HBM per device.

v0:
```python
import jax
import jax.numpy as jnp
from jax import lax
from jax.sharding import PartitionSpec as P


def base_output(tokens, base_projection_weight):
    partial_value = (
        jnp.dot(
            tokens,
            lax.all_gather(base_projection_weight, "dp", axis=1, tiled=True),
            preferred_element_type=jnp.float32,
        )
        .astype(jnp.bfloat16)
        .astype(jnp.float32)
    )
    return lax.psum_scatter(
        partial_value.astype(jnp.bfloat16), "tensor", scatter_dimension=1, tiled=True
    ).astype(jnp.float32)


def adapter_result_rows(tokens, adapter_down_weight, adapter_up_weight, adapter_choice_index):
    row_count, width_portion = tokens.shape
    seq_count = adapter_choice_index.shape[0]
    seq_length = row_count // seq_count
    local_sequence_count = adapter_down_weight.shape[0]
    rank_width_value = adapter_down_weight.shape[2]
    output_portion = adapter_up_weight.shape[2]
    owners = lax.axis_size("adapter")
    capacity = max(2, 6 * seq_count // owners)
    slot_count = owners * capacity
    adapter_list = adapter_choice_index.reshape(-1)
    pair_count = adapter_list.shape[0]
    owner_of = adapter_list // local_sequence_count
    local_index = adapter_list % local_sequence_count
    positions = jnp.arange(pair_count, dtype=jnp.int32)
    earlier = (owner_of[:, None] == owner_of[None, :]) & (positions[None, :] < positions[:, None])
    slot_rank = jnp.sum(earlier.astype(jnp.int32), axis=1)
    slot_of = owner_of * capacity + slot_rank
    select = (jnp.arange(slot_count, dtype=jnp.int32)[:, None] == slot_of[None, :]).astype(
        jnp.bfloat16
    )
    seq_select = select.reshape(slot_count, seq_count, 3).sum(axis=2)
    seq_blocks = tokens.reshape(seq_count, seq_length * width_portion)
    outgoing = jnp.dot(seq_select, seq_blocks, preferred_element_type=jnp.float32).astype(
        jnp.bfloat16
    )
    outgoing = outgoing.reshape(owners, capacity, seq_length, width_portion)
    one_hot = (
        local_index[:, None] == jnp.arange(local_sequence_count, dtype=jnp.int32)[None, :]
    ).astype(jnp.bfloat16)
    adapter_mask = jnp.dot(select, one_hot, preferred_element_type=jnp.float32).astype(jnp.bfloat16)
    adapter_mask = adapter_mask.reshape(owners, capacity, local_sequence_count)
    down_matrix = jnp.transpose(adapter_down_weight, (1, 0, 2)).reshape(
        width_portion, local_sequence_count * rank_width_value
    )
    up_matrix = adapter_up_weight.reshape(local_sequence_count * rank_width_value, output_portion)
    arrived = lax.all_to_all(outgoing, "adapter", split_axis=0, concat_axis=0, tiled=True)
    arrived_mask = lax.all_to_all(adapter_mask, "adapter", split_axis=0, concat_axis=0, tiled=True)
    senders = arrived.shape[0]
    item_count = arrived.shape[1]
    flattened = arrived.reshape(-1, width_portion)
    every_hidden = jnp.dot(flattened, down_matrix, preferred_element_type=jnp.float32)
    every_hidden = every_hidden.reshape(
        senders, item_count, seq_length, local_sequence_count, rank_width_value
    )
    weights_mask = arrived_mask[:, :, None, :, None]
    chosen = jnp.sum(every_hidden * weights_mask.astype(jnp.float32), axis=3)
    summed = lax.psum(chosen.astype(jnp.bfloat16), "tensor")
    spread = (summed[:, :, :, None, :] * weights_mask).reshape(
        -1, local_sequence_count * rank_width_value
    )
    delta_rows = jnp.dot(spread, up_matrix, preferred_element_type=jnp.float32).astype(jnp.bfloat16)
    delta_rows = delta_rows.reshape(senders, item_count, seq_length, output_portion)
    returned = lax.all_to_all(delta_rows, "adapter", split_axis=0, concat_axis=0, tiled=True)
    returned = returned.reshape(slot_count, seq_length * output_portion)
    gathered_sum = jnp.dot(seq_select.T, returned, preferred_element_type=jnp.float32)
    return gathered_sum.reshape(row_count, output_portion)


def local(
    tokens, base_projection_weight, adapter_down_weight, adapter_up_weight, adapter_choice_index
):
    base_sum = base_output(tokens, base_projection_weight)
    adapter_total_sum = adapter_result_rows(
        tokens, adapter_down_weight, adapter_up_weight, adapter_choice_index
    )
    return (base_sum + adapter_total_sum / 3.0).astype(jnp.bfloat16)


def solution(mesh):
    in_specs = (
        P(("adapter", "dp"), "tensor"),
        P("tensor", "dp"),
        P("adapter", "tensor", None),
        P("adapter", None, "tensor"),
        P(("adapter", "dp"), None),
    )
    out_specs = P(("adapter", "dp"), "tensor")
    return jax.shard_map(local, mesh=mesh, in_specs=in_specs, out_specs=out_specs, check_vma=False)
```

profile of v0, /device:TPU:10, one launch (start us, length us, event | category | flops | bytes accessed | tf_op | source)
XLA Modules:
  0.0 355.2 jit_solution(7095717411438507440)
XLA Ops:
  7.4 0.8 copy.37
  8.2 0.1 reshape.149
  8.3 0.2 convert_reduce_fusion
  8.5 0.2 convolution_convert_fusion.3
  8.7 0.1 reshape.153
  8.8 0.6 copy.43
  9.4 15.2 %all-to-all-start.1 = ((bf16[16,3,2]{1,2,0:T(2,128)(2,1)}), bf16[16,3,2]{1,2,0:T(2,128)(2,1)S(1)}, u32[]{:S(2)}, u32[]{:S(2)}) async-start(bf16[16,3,2]{1,2,0:T(2,128)(2,1)} %copy.43), calls=%async_computation.2 | async-start | bytes 16384 | tf_op jit(solution)/shard_map/all_to_all | solution.py:59
  24.7 0.1 copy.42
  24.8 0.1 fusion.8
  24.9 1.3 reshape.150
  26.2 1.0 convolution_convert_fusion
  27.2 3.4 copy.49
  30.6 6.4 %all-to-all-done.1 = bf16[16,3,2]{1,2,0:T(2,128)(2,1)S(1)} async-done(((bf16[16,3,2]{1,2,0:T(2,128)(2,1)}), bf16[16,3,2]{1,2,0:T(2,128)(2,1)S(1)}, u32[]{:S(2)}, u32[]{:S(2)}) %all-to-all-start.1) | async-done | bytes 224 | tf_op jit(solution)/shard_map/all_to_all | solution.py:59
  37.0 5.7 %all-to-all-start = ((bf16[16,3,32,1024]{3,2,1,0:T(8,128)(2,1)}), bf16[16,3,32,1024]{3,2,1,0:T(8,128)(2,1)S(1)}, u32[]{:S(2)}, u32[]{:S(2)}) async-start(bf16[16,3,32,1024]{3,2,1,0:T(8,128)(2,1)} %bitcast.18), calls=%async_computation.1 | async-start | bytes 6291456 | tf_op jit(solution)/shard_map/all_to_all | solution.py:58
  42.7 0.1 copy.44
  42.8 0.1 copy.45
  42.9 139.0 %all-to-all-done = bf16[16,3,32,1024]{3,2,1,0:T(8,128)(2,1)S(1)} async-done(((bf16[16,3,32,1024]{3,2,1,0:T(8,128)(2,1)}), bf16[16,3,32,1024]{3,2,1,0:T(8,128)(2,1)S(1)}, u32[]{:S(2)}, u32[]{:S(2)}) %all-to-all-start) | async-done | bytes 3145760 | tf_op jit(solution)/shard_map/all_to_all | solution.py:58
  181.9 1.8 multiply_reduce_fusion
  183.8 0.5 all-gather.2.cloned.1.call-update
  184.4 0.2 copy.46
  184.6 70.5 %all-reduce.2.cloned.1.call-done = bf16[16,3,32,64]{3,2,1,0:T(8,128)(2,1)} async-done(((bf16[16,3,32,64]{3,2,1,0:T(8,128)(2,1)}), bf16[16,3,32,64]{3,2,1,0:T(8,128)(2,1)}) %all-reduce.2.cloned.1.call-update) | async-done | bytes 196624 | tf_op jit(solution)/shard_map/psum | solution.py:69
  255.1 1.8 broadcast_multiply_fusion
  257.0 0.4 mul.48
  257.4 1.7 convolution_convert_fusion.2
  259.1 12.3 %all-to-all-start.2 = ((bf16[16,3,32,512]{3,2,1,0:T(8,128)(2,1)}), bf16[16,3,32,512]{3,2,1,0:T(8,128)(2,1)S(1)}, u32[]{:S(2)}, u32[]{:S(2)}) async-start(bf16[16,3,32,512]{3,2,1,0:T(8,128)(2,1)} %bitcast.9), calls=%async_computation.3 | async-start | bytes 3145728 | tf_op jit(solution)/shard_map/all_to_all | solution.py:75
  271.4 2.9 all-gather.2.cloned.1.call-done
  274.4 7.1 %convolution_convert_fusion.1 = bf16[256,4096]{1,0:T(8,128)(2,1)} fusion(bf16[256,1024]{1,0:T(8,128)(2,1)S(1)} %copy-done.1, bf16[1024,4096]{1,0:T(8,128)(2,1)} %all-gather.2.cloned.1.call-done), kind=kOutput, calls=%fused_computation.2 | convolution fusion | flops 2148532224 | bytes 11010048 | tf_op jit(solution)/shard_map/dot_general | solution.py:9
  281.5 63.2 %all-to-all-done.2 = bf16[16,3,32,512]{3,2,1,0:T(8,128)(2,1)S(1)} async-done(((bf16[16,3,32,512]{3,2,1,0:T(8,128)(2,1)}), bf16[16,3,32,512]{3,2,1,0:T(8,128)(2,1)S(1)}, u32[]{:S(2)}, u32[]{:S(2)}) %all-to-all-start.2) | async-done | bytes 1572896 | tf_op jit(solution)/shard_map/all_to_all | solution.py:75
  344.7 0.9 copy.50
  345.6 0.3 convolution_multiply_fusion
  345.9 0.1 div.32
  346.1 1.7 add_convert_fusion
  (16 shorter events, 0.3 us)
Async XLA Ops:
  7.4 174.5 %copy-start = (bf16[2,1024,64]{1,2,0:T(8,128)(2,1)S(1)}, bf16[2,1024,64]{1,2,0:T(8,128)(2,1)}, u32[]{:S(2)}) copy-start(bf16[2,1024,64]{1,2,0:T(8,128)(2,1)} %param.7) | copy-start | bytes 786436
  9.4 27.6 %all-to-all-start.1 = ((bf16[16,3,2]{1,2,0:T(2,128)(2,1)}), bf16[16,3,2]{1,2,0:T(2,128)(2,1)S(1)}, u32[]{:S(2)}, u32[]{:S(2)}) async-start(bf16[16,3,2]{1,2,0:T(2,128)(2,1)} %copy.43), calls=%async_computation.2 | async-start | bytes 16384 | tf_op jit(solution)/shard_map/all_to_all | solution.py:59
  37.0 144.9 %all-to-all-start = ((bf16[16,3,32,1024]{3,2,1,0:T(8,128)(2,1)}), bf16[16,3,32,1024]{3,2,1,0:T(8,128)(2,1)S(1)}, u32[]{:S(2)}, u32[]{:S(2)}) async-start(bf16[16,3,32,1024]{3,2,1,0:T(8,128)(2,1)} %bitcast.18), calls=%async_computation.1 | async-start | bytes 6291456 | tf_op jit(solution)/shard_map/all_to_all | solution.py:58
  42.7 212.5 %all-reduce.2.cloned.1.call-start = ((), (), s32[]{:S(2)}) async-start(), calls=%async_computation.6 | async-start | bytes 786432 | tf_op jit(solution)/shard_map/psum | solution.py:69
  183.8 73.6 %copy-start.2 = (bf16[2,64,512]{2,1,0:T(8,128)(2,1)S(1)}, bf16[2,64,512]{2,1,0:T(8,128)(2,1)}, u32[]{:S(2)}) copy-start(bf16[2,64,512]{2,1,0:T(8,128)(2,1)} %param.8) | copy-start | bytes 393220
  183.8 90.6 %all-gather.2.cloned.1.call-start = ((), (), s32[]{:S(2)}) async-start(), calls=%async_computation.4 | async-start | bytes 10485760 | tf_op jit(solution)/shard_map/all_gather | solution.py:11
  257.0 17.4 %copy-start.1 = (bf16[256,1024]{1,0:T(8,128)(2,1)S(1)}, bf16[256,1024]{1,0:T(8,128)(2,1)}, u32[]{:S(2)}) copy-start(bf16[256,1024]{1,0:T(8,128)(2,1)} %param.5) | copy-start | bytes 1572868
  259.1 85.6 %all-to-all-start.2 = ((bf16[16,3,32,512]{3,2,1,0:T(8,128)(2,1)}), bf16[16,3,32,512]{3,2,1,0:T(8,128)(2,1)S(1)}, u32[]{:S(2)}, u32[]{:S(2)}) async-start(bf16[16,3,32,512]{3,2,1,0:T(8,128)(2,1)} %bitcast.9), calls=%async_computation.3 | async-start | bytes 3145728 | tf_op jit(solution)/shard_map/all_to_all | solution.py:75
  271.4 74.7 %reduce-scatter.2.cloned.1.call-start = ((), (), s32[]{:S(2)}) async-start(), calls=%async_computation.5 | async-start | bytes 2359296 | tf_op jit(solution)/shard_map/reduce_scatter | solution.py:17
Sparse Core Ops, SparseCore 0:
  183.9 71.1 all-reduce.1
  281.6 39.4 reduce-scatter.1
Sparse Core Ops, SparseCore 1:
  186.6 87.7 all-gather.1
where the time goes:
time: 356 us; the launch traced here: 355 us
  waiting for transfers between devices  283 us (79%)
  starting transfers between devices  33.3 us (9%)
  between operations  15 us (4%)
  matrix products  12.2 us (3%)
  local copies, waits for them, and re-layouts  8.26 us (2%)
  other arithmetic  3.87 us (1%)
    all_to_all x1, waiting for transfers between devices, adapter_result_rows(): lax.all_to_all(outgoing, 'adapter', split_axis=0, concat_axis=0, tiled=True)  139 us
    psum x1, waiting for transfers between devices, adapter_result_rows(): summed = lax.psum(chosen.astype(jnp.bfloat16), 'tensor')  70.5 us
    all_to_all x1, waiting for transfers between devices, adapter_result_rows(): lax.all_to_all(delta_rows, 'adapter', split_axis=0, concat_axis=0, tiled=...  63.2 us
    all_to_all x1, starting transfers between devices, adapter_result_rows(): lax.all_to_all(adapter_mask, 'adapter', split_axis=0, concat_axis=0, tile...  15.2 us
    all_to_all x1, starting transfers between devices, adapter_result_rows(): lax.all_to_all(delta_rows, 'adapter', split_axis=0, concat_axis=0, tiled=...  12.3 us
  transfers between devices with their start and end apart: 6, of which 5 were waited for; matrix products, arithmetic and copies ran while one was open for 5% of the time, Pallas kernels for 0%

commit v1 on v0

--- a/solution.py
+++ b/solution.py
@@ -66,7 +66,7 @@
     )
     weights_mask = arrived_mask[:, :, None, :, None]
     chosen = jnp.sum(every_hidden * weights_mask.astype(jnp.float32), axis=3)
-    summed = lax.psum(chosen.astype(jnp.bfloat16), "tensor")
+    summed = jnp.sum(lax.all_gather(chosen.astype(jnp.bfloat16), "tensor"), axis=0)
     spread = (summed[:, :, :, None, :] * weights_mask).reshape(
         -1, local_sequence_count * rank_width_value
     )

time: 356 us -> 367 us (1.031)
  the two profiles are of different devices: /device:TPU:10 before, /device:TPU:2 now
where the time goes in v1:
time: 367 us
  waiting for transfers between devices  294 us (80%)
  starting transfers between devices  33.3 us (9%)
  between operations  13.2 us (4%)
  matrix products  12.2 us (3%)
  local copies, waits for them, and re-layouts  8.26 us (2%)
  other arithmetic  5.54 us (2%)
    all_to_all x1, waiting for transfers between devices, adapter_result_rows(): lax.all_to_all(outgoing, 'adapter', split_axis=0, concat_axis=0, tiled=True)  139 us
    all_gather x1, waiting for transfers between devices, base_output(): lax.all_gather(base_projection_weight, 'dp', axis=1, tiled=True)  75 us
    reduce_scatter x1, waiting for transfers between devices, base_output(): lax.psum_scatter(partial_value.astype(jnp.bfloat16), 'tensor', scatter_di...  41.2 us
    all_gather x1, waiting for transfers between devices, adapter_result_rows(): lax.all_gather(chosen.astype(jnp.bfloat16), 'tensor')  31.9 us
    all_to_all x1, starting transfers between devices, adapter_result_rows(): lax.all_to_all(adapter_mask, 'adapter', split_axis=0, concat_axis=0, tile...  15.2 us
    all_to_all x1, starting transfers between devices, adapter_result_rows(): lax.all_to_all(delta_rows, 'adapter', split_axis=0, concat_axis=0, tiled=...  12.3 us
  transfers between devices with their start and end apart: 6, of which 5 were waited for; matrix products, arithmetic and copies ran while one was open for 6% of the time, Pallas kernels for 0%

profile of v1, /device:TPU:2, one launch (start us, length us, event | category | flops | bytes accessed | tf_op | source)
XLA Modules:
  0.0 366.7 jit_solution(580489176373661283)
XLA Ops:
  6.5 0.8 copy.37
  7.3 0.1 reshape.157
  7.4 0.2 convert_reduce_fusion
  7.6 0.2 convolution_convert_fusion.3
  7.9 0.1 reshape.161
  8.0 0.6 copy.43
  8.6 15.2 %all-to-all-start.1 = ((bf16[16,3,2]{1,2,0:T(2,128)(2,1)}), bf16[16,3,2]{1,2,0:T(2,128)(2,1)S(1)}, u32[]{:S(2)}, u32[]{:S(2)}) async-start(bf16[16,3,2]{1,2,0:T(2,128)(2,1)} %copy.43), calls=%async_computation.2 | async-start | bytes 16384 | tf_op jit(solution)/shard_map/all_to_all | solution.py:59
  23.9 0.1 copy.42
  24.1 1.3 reshape.158
  25.4 1.0 convolution_convert_fusion
  26.4 3.4 copy.49
  29.8 6.4 %all-to-all-done.1 = bf16[16,3,2]{1,2,0:T(2,128)(2,1)S(1)} async-done(((bf16[16,3,2]{1,2,0:T(2,128)(2,1)}), bf16[16,3,2]{1,2,0:T(2,128)(2,1)S(1)}, u32[]{:S(2)}, u32[]{:S(2)}) %all-to-all-start.1) | async-done | bytes 224 | tf_op jit(solution)/shard_map/all_to_all | solution.py:59
  36.2 5.7 %all-to-all-start = ((bf16[16,3,32,1024]{3,2,1,0:T(8,128)(2,1)}), bf16[16,3,32,1024]{3,2,1,0:T(8,128)(2,1)S(1)}, u32[]{:S(2)}, u32[]{:S(2)}) async-start(bf16[16,3,32,1024]{3,2,1,0:T(8,128)(2,1)} %bitcast.19), calls=%async_computation.1 | async-start | bytes 6291456 | tf_op jit(solution)/shard_map/all_to_all | solution.py:58
  41.9 0.1 copy.44
  42.0 0.1 copy.45
  42.1 139.0 %all-to-all-done = bf16[16,3,32,1024]{3,2,1,0:T(8,128)(2,1)S(1)} async-done(((bf16[16,3,32,1024]{3,2,1,0:T(8,128)(2,1)}), bf16[16,3,32,1024]{3,2,1,0:T(8,128)(2,1)S(1)}, u32[]{:S(2)}, u32[]{:S(2)}) %all-to-all-start) | async-done | bytes 3145760 | tf_op jit(solution)/shard_map/all_to_all | solution.py:58
  181.1 1.8 multiply_reduce_fusion
  182.9 0.7 all-gather.4.cloned.1.call-update
  183.7 0.2 copy.46
  183.9 31.9 %all-gather.6.cloned.1.call-done = bf16[128,3,32,64]{3,2,1,0:T(8,128)(2,1)} async-done(((bf16[16,3,32,64]{3,2,1,0:T(8,128)(2,1)}), bf16[128,3,32,64]{3,2,1,0:T(8,128)(2,1)}) %all-gather.6.cloned.1.call-update) | async-done | bytes 1572880 | tf_op jit(solution)/shard_map/all_gather | solution.py:69
  215.7 2.7 reduce_sum.48
  218.4 0.8 broadcast_multiply_fusion
  219.3 0.4 mul.48
  219.6 1.7 convolution_convert_fusion.2
  221.3 12.3 %all-to-all-start.2 = ((bf16[16,3,32,512]{3,2,1,0:T(8,128)(2,1)}), bf16[16,3,32,512]{3,2,1,0:T(8,128)(2,1)S(1)}, u32[]{:S(2)}, u32[]{:S(2)}) async-start(bf16[16,3,32,512]{3,2,1,0:T(8,128)(2,1)} %bitcast.10), calls=%async_computation.3 | async-start | bytes 3145728 | tf_op jit(solution)/shard_map/all_to_all | solution.py:75
  233.7 75.0 %all-gather.4.cloned.1.call-done = bf16[1024,4096]{1,0:T(8,128)(2,1)} async-done(((bf16[1024,1024]{1,0:T(8,128)(2,1)}), bf16[1024,4096]{1,0:T(8,128)(2,1)}) %all-gather.4.cloned.1.call-update) | async-done | bytes 8388624 | tf_op jit(solution)/shard_map/all_gather | solution.py:11
  308.7 7.1 %convolution_convert_fusion.1 = bf16[256,4096]{1,0:T(8,128)(2,1)} fusion(bf16[256,1024]{1,0:T(8,128)(2,1)S(1)} %copy-done.1, bf16[1024,4096]{1,0:T(8,128)(2,1)} %all-gather.4.cloned.1.call-done), kind=kOutput, calls=%fused_computation.2 | convolution fusion | flops 2148532224 | bytes 11010048 | tf_op jit(solution)/shard_map/dot_general | solution.py:9
  315.9 0.9 copy.50
  316.8 0.3 convolution_multiply_fusion
  317.1 0.1 div.32
  317.2 41.2 %reduce-scatter.2.cloned.1.call-done = bf16[256,512]{1,0:T(8,128)(2,1)} async-done(((bf16[256,4096]{1,0:T(8,128)(2,1)}), bf16[256,512]{1,0:T(8,128)(2,1)}) %reduce-scatter.2.cloned.1.call-update) | async-done | bytes 262160 | tf_op jit(solution)/shard_map/reduce_scatter | solution.py:17
  358.4 1.7 add_convert_fusion
  (17 shorter events, 0.4 us)
Async XLA Ops:
  6.5 174.5 %copy-start = (bf16[2,1024,64]{1,2,0:T(8,128)(2,1)S(1)}, bf16[2,1024,64]{1,2,0:T(8,128)(2,1)}, u32[]{:S(2)}) copy-start(bf16[2,1024,64]{1,2,0:T(8,128)(2,1)} %param.7) | copy-start | bytes 786436
  8.6 27.6 %all-to-all-start.1 = ((bf16[16,3,2]{1,2,0:T(2,128)(2,1)}), bf16[16,3,2]{1,2,0:T(2,128)(2,1)S(1)}, u32[]{:S(2)}, u32[]{:S(2)}) async-start(bf16[16,3,2]{1,2,0:T(2,128)(2,1)} %copy.43), calls=%async_computation.2 | async-start | bytes 16384 | tf_op jit(solution)/shard_map/all_to_all | solution.py:59
  36.2 144.9 %all-to-all-start = ((bf16[16,3,32,1024]{3,2,1,0:T(8,128)(2,1)}), bf16[16,3,32,1024]{3,2,1,0:T(8,128)(2,1)S(1)}, u32[]{:S(2)}, u32[]{:S(2)}) async-start(bf16[16,3,32,1024]{3,2,1,0:T(8,128)(2,1)} %bitcast.19), calls=%async_computation.1 | async-start | bytes 6291456 | tf_op jit(solution)/shard_map/all_to_all | solution.py:58
  41.8 173.9 %all-gather.6.cloned.1.call-start = ((), (), s32[]{:S(2)}) async-start(), calls=%async_computation.6 | async-start | bytes 3538944 | tf_op jit(solution)/shard_map/all_gather | solution.py:69
  182.9 125.8 %all-gather.4.cloned.1.call-start = ((), (), s32[]{:S(2)}) async-start(), calls=%async_computation.4 | async-start | bytes 10485760 | tf_op jit(solution)/shard_map/all_gather | solution.py:11
  183.6 36.0 %copy-start.2 = (bf16[2,64,512]{2,1,0:T(8,128)(2,1)S(1)}, bf16[2,64,512]{2,1,0:T(8,128)(2,1)}, u32[]{:S(2)}) copy-start(bf16[2,64,512]{2,1,0:T(8,128)(2,1)} %param.8) | copy-start | bytes 393220
  219.3 89.5 %copy-start.1 = (bf16[256,1024]{1,0:T(8,128)(2,1)S(1)}, bf16[256,1024]{1,0:T(8,128)(2,1)}, u32[]{:S(2)}) copy-start(bf16[256,1024]{1,0:T(8,128)(2,1)} %param.5) | copy-start | bytes 1572868
  221.3 94.5 %all-to-all-start.2 = ((bf16[16,3,32,512]{3,2,1,0:T(8,128)(2,1)}), bf16[16,3,32,512]{3,2,1,0:T(8,128)(2,1)S(1)}, u32[]{:S(2)}, u32[]{:S(2)}) async-start(bf16[16,3,32,512]{3,2,1,0:T(8,128)(2,1)} %bitcast.10), calls=%async_computation.3 | async-start | bytes 3145728 | tf_op jit(solution)/shard_map/all_to_all | solution.py:75
  233.6 124.8 %reduce-scatter.2.cloned.1.call-start = ((), (), s32[]{:S(2)}) async-start(), calls=%async_computation.5 | async-start | bytes 2359296 | tf_op jit(solution)/shard_map/reduce_scatter | solution.py:17
Sparse Core Ops, SparseCore 0:
  183.0 32.6 all-gather.5
  217.8 90.8 all-gather.3
  316.0 42.3 reduce-scatter.1
